TPU v7x, 256 devices: a whole 4x4x8 slice. The times are simulated.
256 devices in a mesh: row: 16 (over x, y_lo, core), col: 8 (over z), slab: 2 (over y_hi).
Axes of the slice: x: 4, y: 4 (y_hi: 2, y_lo: 2; y = y_hi * 2 + y_lo), z: 8, core: 2. Of those that a mesh axis runs over, the one named last changes fastest.
Arguments:
- fields: bfloat16 [2, 16384, 1024], P(None, ('row', 'col', 'slab')), may hold values from -0.8984375 to 0.8984375
Outputs:
- gram: float32 [2, 16384, 16384], P(None, ('row', 'slab'), 'col')
All inputs are finite; a program needn't handle non-finite values.
Results may differ from a plain program's by a relative error of at most 0.01.
Values may be sent and summed in bfloat16 or wider, within the bound.
A program may use at most 64 MiB of HBM per device.

v0:
```python
import jax
import jax.numpy as jnp
from jax import lax
from jax.sharding import PartitionSpec as P


def pair_terms(left_real, left_imag, piece):
    right_real = jnp.concatenate([piece[0], piece[1]], axis=1)
    right_imag = jnp.concatenate([piece[1], piece[0]], axis=1)
    dims = (((1,), (1,)), ((), ()))
    real = lax.dot_general(left_real, right_real, dims, preferred_element_type=jnp.float32)
    imag = lax.dot_general(left_imag, right_imag, dims, preferred_element_type=jnp.float32)
    return jnp.stack([real, imag])


def body(fields):
    local = lax.all_to_all(fields, "slab", split_axis=2, concat_axis=1, tiled=True)
    row_block = lax.all_gather(local, "col", axis=1, tiled=True)
    left_real = jnp.concatenate([row_block[0], row_block[1]], axis=1)
    left_imag = jnp.concatenate([row_block[0], -row_block[1]], axis=1)
    column_set = lax.all_gather(local, "row", axis=1, tiled=True)
    terms = pair_terms(left_real, left_imag, column_set)
    gram = lax.psum_scatter(
        terms.astype(jnp.bfloat16), "slab", scatter_dimension=1, tiled=True
    ).astype(jnp.float32)
    return gram


def solution(mesh):
    placed = (P(None, ("row", "col", "slab"), None),)
    return jax.shard_map(
        body, mesh=mesh, in_specs=placed, out_specs=P(None, ("row", "slab"), "col"), check_vma=False
    )
```

profile of v0, /device:TPU:1, one launch (start us, length us, event | category | flops | bytes accessed | tf_op | source)
XLA Modules:
  0.0 242.6 jit_solution(3190334933049715580)
XLA Ops:
  6.5 0.0 all-gather.3.cloned.1.call-start
  6.5 1.3 copy.3
  7.8 0.4 reshape
  8.2 10.3 %all_to_all.18 = bf16[2,2,32768]{2,1,0:T(2,128)(2,1)S(1)} all-to-all(bf16[2,2,32768]{2,1,0:T(2,128)(2,1)S(1)} %reshape), channel_id=1, replica_groups=mesh['row'=16,'col'=8,'slab'=2] {'slab'}, dimensions={0} | all-to-all | bytes 524288 | tf_op jit(solution)/shard_map/all_to_all | solution.py:17
  18.6 0.3 reshape.1
  18.9 1.0 copy.5
  19.9 0.0 all-gather.3.cloned.1.call-update
  19.9 0.0 all-gather.5.cloned.1.call-start
  20.0 0.7 all-gather.5.cloned.1.call-update
  20.7 0.0 reduce-scatter.2.cloned.1.call-start
  20.7 38.7 %all-gather.3.cloned.1.call-done = bf16[2,1024,512]{2,1,0:T(8,128)(2,1)} async-done(((bf16[2,128,512]{2,1,0:T(8,128)(2,1)}), bf16[2,1024,512]{2,1,0:T(8,128)(2,1)}) %all-gather.3.cloned.1.call-update) | async-done | bytes 2097168 | tf_op jit(solution)/shard_map/all_gather | solution.py:18
  59.4 1.3 fusion.16
  60.7 2.6 %slice_bitcast_fusion.2 = (bf16[1024,512]{1,0:T(8,128)(2,1)}, bf16[1024,512]{1,0:T(8,128)(2,1)S(1)}) fusion(bf16[2,1024,512]{2,1,0:T(8,128)(2,1)} %all-gather.3.cloned.1.call-done), kind=kLoop, calls=%fused_computation.17 | loop fusion | bytes 4194304 | tf_op jit(solution)/shard_map/squeeze | solution.py:19
  63.3 40.4 %all-gather.5.cloned.1.call-done = bf16[2,2048,512]{2,1,0:T(8,128)(2,1)} async-done(((bf16[2,128,512]{2,1,0:T(8,128)(2,1)}), bf16[2,2048,512]{2,1,0:T(8,128)(2,1)}) %all-gather.5.cloned.1.call-update) | async-done | bytes 4194320 | tf_op jit(solution)/shard_map/all_gather | solution.py:21
  103.8 0.0 copy-start
  103.8 2.6 %slice_bitcast_fusion = (bf16[2048,512]{1,0:T(8,128)(2,1)S(1)}, bf16[2048,512]{1,0:T(8,128)(2,1)S(1)}) fusion(bf16[2,2048,512]{2,1,0:T(8,128)(2,1)} %all-gather.5.cloned.1.call-done), kind=kLoop, calls=%fused_computation.13 | loop fusion | bytes 8388608 | tf_op jit(solution)/shard_map/squeeze | solution.py:8
  106.3 0.0 copy-done
  106.3 4.8 %convert_bitcast_fusion.1 = bf16[1,1024,2048]{2,1,0:T(8,128)(2,1)S(1)} fusion(bf16[2048,512]{1,0:T(8,128)(2,1)S(1)} %get-tuple-element.5, bf16[2048,512]{1,0:T(8,128)(2,1)S(1)} %get-tuple-element.6, bf16[1024,512]{1,0:T(8,128)(2,1)S(1)} %get-tuple-element.8, bf16[1024,512]{1,0:T(8,128)(2,1)S(1)} %copy-done), kind=kOutput, calls=%fused_computation.10 | convolution fusion | flops 4309647360 | bytes 10485760 | tf_op jit(solution)/shard_map/dot_general | solution.py:11
  111.1 6.1 %convert_bitcast_fusion = bf16[1,1024,2048]{2,1,0:T(8,128)(2,1)} fusion(bf16[2048,512]{1,0:T(8,128)(2,1)S(1)} %get-tuple-element.6, bf16[2048,512]{1,0:T(8,128)(2,1)S(1)} %get-tuple-element.5, bf16[1024,512]{1,0:T(8,128)(2,1)S(1)} %get-tuple-element.8, bf16[1024,512]{1,0:T(8,128)(2,1)S(1)} %fusion.16), kind=kOutput, calls=%fused_computation.9 | convolution fusion | flops 4309647360 | bytes 10485760 | tf_op jit(solution)/shard_map/dot_general | solution.py:12
  117.3 6.3 %pad_maximum_fusion = bf16[2,1024,2048]{2,1,0:T(8,128)(2,1)} fusion(bf16[1,1024,2048]{2,1,0:T(8,128)(2,1)} %convert_bitcast_fusion, bf16[1,1024,2048]{2,1,0:T(8,128)(2,1)S(1)} %convert_bitcast_fusion.1), kind=kLoop, calls=%fused_computation | loop fusion | flops 4194304 | bytes 16777216 | tf_op jit(solution)/shard_map/stack | solution.py:13
  123.6 0.0 reduce-scatter.2.cloned.1.call-update
  123.6 105.7 %reduce-scatter.2.cloned.1.call-done = bf16[2,512,2048]{2,1,0:T(8,128)(2,1)} async-done(((bf16[2,1024,2048]{2,1,0:T(8,128)(2,1)}), bf16[2,512,2048]{2,1,0:T(8,128)(2,1)}) %reduce-scatter.2.cloned.1.call-update) | async-done | bytes 4194320 | tf_op jit(solution)/shard_map/reduce_scatter | solution.py:23
  229.4 6.7 %convert_element_type.4 = f32[2,512,2048]{2,1,0:T(8,128)} convert(bf16[2,512,2048]{2,1,0:T(8,128)(2,1)} %reduce-scatter.2.cloned.1.call-done) | non-fusion elementwise | flops 2097152 | bytes 12582912 | tf_op jit(solution)/shard_map/convert_element_type | solution.py:25
Async XLA Ops:
  6.5 52.9 %all-gather.3.cloned.1.call-start = ((), (), s32[]{:S(2)}) async-start(), calls=%async_computation.2 | async-start | bytes 2359296 | tf_op jit(solution)/shard_map/all_gather | solution.py:18
  19.9 83.8 %all-gather.5.cloned.1.call-start = ((), (), s32[]{:S(2)}) async-start(), calls=%async_computation.3 | async-start | bytes 4456448 | tf_op jit(solution)/shard_map/all_gather | solution.py:21
  20.7 208.7 %reduce-scatter.2.cloned.1.call-start = ((), (), s32[]{:S(2)}) async-start(), calls=%async_computation.4 | async-start | bytes 12582912 | tf_op jit(solution)/shard_map/reduce_scatter | solution.py:23
  103.8 2.6 %copy-start = (bf16[1024,512]{1,0:T(8,128)(2,1)S(1)}, bf16[1024,512]{1,0:T(8,128)(2,1)}, u32[]{:S(2)}) copy-start(bf16[1024,512]{1,0:T(8,128)(2,1)} %get-tuple-element.7) | copy-start | bytes 3145732
Sparse Core Ops, SparseCore 0:
  20.1 39.2 all-gather.2
  61.2 42.4 all-gather.4
  123.8 105.5 reduce-scatter.1
where the time goes:
time: 243 us
  waiting for transfers between devices  186 us (77%)
  other arithmetic  14.3 us (6%)
  between operations  13.2 us (5%)
  matrix products  10.9 us (4%)
  blocking collectives  10.3 us (4%)
  local copies, waits for them, and re-layouts  8.25 us (3%)
    reduce_scatter x1, waiting for transfers between devices, body(): lax.psum_scatter(terms.astype(jnp.bfloat16), 'slab', scatter_dimension=1,...  106 us
    all_gather x1, waiting for transfers between devices, body(): column_set = lax.all_gather(local, 'row', axis=1, tiled=True)  40.4 us
    all_gather x1, waiting for transfers between devices, body(): row_block = lax.all_gather(local, 'col', axis=1, tiled=True)  38.7 us
    all_to_all x1, blocking collectives, body(): lax.all_to_all(fields, 'slab', split_axis=2, concat_axis=1, tiled=True)  10.3 us
    convert_element_type x1, other arithmetic, body(): gram = lax.psum_scatter(terms.astype(jnp.bfloat16), 'slab', scatter_dimen...  6.65 us
    another operation x1, other arithmetic, pair_terms(): return jnp.stack([real, imag])  6.35 us
    dot_general x1, matrix products, pair_terms(): lax.dot_general(left_imag, right_imag, dims, preferred_element_type=jnp.f...  6.13 us
  transfers between devices with their start and end apart: 3, of which 3 were waited for; matrix products, arithmetic and copies ran while one was open for 2% of the time, Pallas kernels for 0%

commit v1 on v0

--- a/solution.py
+++ b/solution.py
@@ -18,7 +18,12 @@
     row_block = lax.all_gather(local, "col", axis=1, tiled=True)
     left_real = jnp.concatenate([row_block[0], row_block[1]], axis=1)
     left_imag = jnp.concatenate([row_block[0], -row_block[1]], axis=1)
-    column_set = lax.all_gather(local, "row", axis=1, tiled=True)
+    column_set = jnp.concatenate(
+        lax.all_to_all(
+            jnp.stack([local for _ in range(lax.axis_size("row"))], axis=0), "row", 0, 0
+        ),
+        1,
+    )
     terms = pair_terms(left_real, left_imag, column_set)
     gram = lax.psum_scatter(
         terms.astype(jnp.bfloat16), "slab", scatter_dimension=1, tiled=True

time: 243 us -> 229 us (0.942)
  waiting for transfers between devices: 186 us -> 162 us
  starting transfers between devices: 0.08 us -> 6.57 us
  local copies, waits for them, and re-layouts: 8.25 us -> 11.7 us
    all_gather x1 -> x0, waiting for transfers between devices: 40.4 us -> none  [body(): column_set = lax.all_gather(local, 'row', axis=1, tiled=True)]
    all_to_all x0 -> x1, waiting for transfers between devices: none -> 19.3 us  [body(): lax.all_to_all(jnp.stack([local for _ in range(lax.axis_size('row'))], ax...]
    all_gather x1, waiting for transfers between devices: 38.7 us -> 29.4 us  [body(): row_block = lax.all_gather(local, 'col', axis=1, tiled=True)]
    reduce_scatter x1, waiting for transfers between devices: 106 us -> 113 us  [body(): lax.psum_scatter(terms.astype(jnp.bfloat16), 'slab', scatter_dimension=1,...]
    all_to_all x0 -> x1, starting transfers between devices: none -> 6.53 us  [body(): lax.all_to_all(jnp.stack([local for _ in range(lax.axis_size('row'))], ax...]
    another operation x0 -> x1, local copies, waits for them, and re-layouts: none -> 3.44 us  [body(): jnp.stack([local for _ in range(lax.axis_size('row'))], axis=0)]
    slice x0 -> x1, local copies, waits for them, and re-layouts: none -> 2.58 us  [pair_terms(): right_real = jnp.concatenate([piece[0], piece[1]], axis=1)]
    squeeze x1 -> x0, local copies, waits for them, and re-layouts: 2.58 us -> none  [pair_terms(): right_real = jnp.concatenate([piece[0], piece[1]], axis=1)]
  transfers between devices with their start and end apart: 3 -> 3, of which waited for: 3 -> 3; matrix products, arithmetic and copies ran while one was open for 2% -> 3% of each run, Pallas kernels for 0% -> 0%
where the time goes in v1:
time: 229 us
  waiting for transfers between devices  162 us (71%)
  other arithmetic  14.3 us (6%)
  between operations  13.4 us (6%)
  local copies, waits for them, and re-layouts  11.7 us (5%)
  matrix products  10.9 us (5%)
  blocking collectives  10.3 us (4%)
  starting transfers between devices  6.57 us (3%)
    reduce_scatter x1, waiting for transfers between devices, body(): lax.psum_scatter(terms.astype(jnp.bfloat16), 'slab', scatter_dimension=1,...  113 us
    all_gather x1, waiting for transfers between devices, body(): row_block = lax.all_gather(local, 'col', axis=1, tiled=True)  29.4 us
    all_to_all x1, waiting for transfers between devices, body(): lax.all_to_all(jnp.stack([local for _ in range(lax.axis_size('row'))], ax...  19.3 us
    all_to_all x1, blocking collectives, body(): lax.all_to_all(fields, 'slab', split_axis=2, concat_axis=1, tiled=True)  10.3 us
    convert_element_type x1, other arithmetic, body(): gram = lax.psum_scatter(terms.astype(jnp.bfloat16), 'slab', scatter_dimen...  6.65 us
    all_to_all x1, starting transfers between devices, body(): lax.all_to_all(jnp.stack([local for _ in range(lax.axis_size('row'))], ax...  6.53 us
    another operation x1, other arithmetic, pair_terms(): return jnp.stack([real, imag])  6.35 us
    dot_general x1, matrix products, pair_terms(): lax.dot_general(left_real, right_real, dims, preferred_element_type=jnp.f...  6.11 us
  transfers between devices with their start and end apart: 3, of which 3 were waited for; matrix products, arithmetic and copies ran while one was open for 3% of the time, Pallas kernels for 0%

profile of v1, /device:TPU:1, one launch (start us, length us, event | category | flops | bytes accessed | tf_op | source)
XLA Modules:
  0.0 228.8 jit_solution(15045254659983773219)
XLA Ops:
  6.5 0.0 all-gather.2.cloned.1.call-start
  6.5 1.3 copy.3
  7.8 0.4 reshape.12
  8.2 10.3 %all_to_all.23 = bf16[2,2,32768]{2,1,0:T(2,128)(2,1)S(1)} all-to-all(bf16[2,2,32768]{2,1,0:T(2,128)(2,1)S(1)} %reshape.12), channel_id=1, replica_groups=mesh['row'=16,'col'=8,'slab'=2] {'slab'}, dimensions={0} | all-to-all | bytes 524288 | tf_op jit(solution)/shard_map/all_to_all | solution.py:17
  18.6 0.3 reshape.13
  18.9 1.0 copy.5
  19.9 0.0 all-gather.2.cloned.1.call-update
  20.0 3.4 %stack.11 = bf16[16,2,128,512]{3,2,1,0:T(8,128)(2,1)} broadcast(bf16[2,128,512]{2,1,0:T(8,128)(2,1)} %bitcast.21), dimensions={1,2,3} | broadcast | bytes 4456448 | tf_op jit(solution)/shard_map/stack | solution.py:23
  23.4 6.5 %all-to-all-start.1 = ((bf16[16,2,128,512]{3,2,1,0:T(8,128)(2,1)}), bf16[16,2,128,512]{3,2,1,0:T(8,128)(2,1)}, u32[]{:S(2)}, u32[]{:S(2)}) async-start(bf16[16,2,128,512]{3,2,1,0:T(8,128)(2,1)} %stack.11), calls=%async_computation.1 | async-start | bytes 8388608 | tf_op jit(solution)/shard_map/all_to_all | solution.py:22
  29.9 0.0 reduce-scatter.2.cloned.1.call-start
  30.0 29.4 %all-gather.2.cloned.1.call-done = bf16[2,1024,512]{2,1,0:T(8,128)(2,1)} async-done(((bf16[2,128,512]{2,1,0:T(8,128)(2,1)}), bf16[2,1024,512]{2,1,0:T(8,128)(2,1)}) %all-gather.2.cloned.1.call-update) | async-done | bytes 2097168 | tf_op jit(solution)/shard_map/all_gather | solution.py:18
  59.4 1.3 fusion.16
  60.7 2.7 %slice_bitcast_fusion = (bf16[1024,512]{1,0:T(8,128)(2,1)S(1)}, bf16[1024,512]{1,0:T(8,128)(2,1)}) fusion(bf16[2,1024,512]{2,1,0:T(8,128)(2,1)} %all-gather.2.cloned.1.call-done), kind=kLoop, calls=%fused_computation.15 | loop fusion | bytes 4194304 | tf_op jit(solution)/shard_map/squeeze | solution.py:19
  63.4 19.3 %all-to-all-done.1 = bf16[16,2,128,512]{3,2,1,0:T(8,128)(2,1)} async-done(((bf16[16,2,128,512]{3,2,1,0:T(8,128)(2,1)}), bf16[16,2,128,512]{3,2,1,0:T(8,128)(2,1)}, u32[]{:S(2)}, u32[]{:S(2)}) %all-to-all-start.1) | async-done | bytes 4194336 | tf_op jit(solution)/shard_map/all_to_all | solution.py:22
  82.6 0.0 copy-start
  82.6 2.6 %fusion.17 = (bf16[1,16,128,512]{3,2,0,1:T(8,128)(2,1)S(1)}, bf16[1,16,128,512]{3,2,0,1:T(8,128)(2,1)S(1)}) fusion(bf16[2,16,128,512]{3,2,0,1:T(8,128)(2,1)} %bitcast.7), kind=kLoop, calls=%fused_computation.20 | loop fusion | bytes 8388608 | tf_op jit(solution)/shard_map/slice | solution.py:8
  85.2 0.0 copy-done
  85.2 4.8 %convert_bitcast_fusion = bf16[1,1024,2048]{2,1,0:T(8,128)(2,1)S(1)} fusion(bf16[2048,512]{1,0:T(8,128)(2,1)S(1)} %bitcast.26, bf16[2048,512]{1,0:T(8,128)(2,1)S(1)} %bitcast.24, bf16[1024,512]{1,0:T(8,128)(2,1)S(1)} %copy-done, bf16[1024,512]{1,0:T(8,128)(2,1)S(1)} %fusion.16), kind=kOutput, calls=%fused_computation.9 | convolution fusion | flops 4309647360 | bytes 10485760 | tf_op jit(solution)/shard_map/dot_general | solution.py:12
  90.0 6.1 %convert_bitcast_fusion.1 = bf16[1,1024,2048]{2,1,0:T(8,128)(2,1)} fusion(bf16[2048,512]{1,0:T(8,128)(2,1)S(1)} %bitcast.25, bf16[2048,512]{1,0:T(8,128)(2,1)S(1)} %bitcast.27, bf16[1024,512]{1,0:T(8,128)(2,1)S(1)} %copy-done, bf16[1024,512]{1,0:T(8,128)(2,1)S(1)} %get-tuple-element.7), kind=kOutput, calls=%fused_computation.10 | convolution fusion | flops 4309647360 | bytes 10485760 | tf_op jit(solution)/shard_map/dot_general | solution.py:11
  96.1 6.3 %pad_maximum_fusion = bf16[2,1024,2048]{2,1,0:T(8,128)(2,1)} fusion(bf16[1,1024,2048]{2,1,0:T(8,128)(2,1)S(1)} %convert_bitcast_fusion, bf16[1,1024,2048]{2,1,0:T(8,128)(2,1)} %convert_bitcast_fusion.1), kind=kLoop, calls=%fused_computation | loop fusion | flops 4194304 | bytes 16777216 | tf_op jit(solution)/shard_map/stack | solution.py:13
  102.5 0.0 reduce-scatter.2.cloned.1.call-update
  102.5 112.8 %reduce-scatter.2.cloned.1.call-done = bf16[2,512,2048]{2,1,0:T(8,128)(2,1)} async-done(((bf16[2,1024,2048]{2,1,0:T(8,128)(2,1)}), bf16[2,512,2048]{2,1,0:T(8,128)(2,1)}) %reduce-scatter.2.cloned.1.call-update) | async-done | bytes 4194320 | tf_op jit(solution)/shard_map/reduce_scatter | solution.py:28
  215.3 6.7 %convert_element_type.4 = f32[2,512,2048]{2,1,0:T(8,128)} convert(bf16[2,512,2048]{2,1,0:T(8,128)(2,1)} %reduce-scatter.2.cloned.1.call-done) | non-fusion elementwise | flops 2097152 | bytes 12582912 | tf_op jit(solution)/shard_map/convert_element_type | solution.py:30
Async XLA Ops:
  6.5 52.9 %all-gather.2.cloned.1.call-start = ((), (), s32[]{:S(2)}) async-start(), calls=%async_computation.3 | async-start | bytes 2359296 | tf_op jit(solution)/shard_map/all_gather | solution.py:18
  23.4 59.3 %all-to-all-start.1 = ((bf16[16,2,128,512]{3,2,1,0:T(8,128)(2,1)}), bf16[16,2,128,512]{3,2,1,0:T(8,128)(2,1)}, u32[]{:S(2)}, u32[]{:S(2)}) async-start(bf16[16,2,128,512]{3,2,1,0:T(8,128)(2,1)} %stack.11), calls=%async_computation.1 | async-start | bytes 8388608 | tf_op jit(solution)/shard_map/all_to_all | solution.py:22
  29.9 185.4 %reduce-scatter.2.cloned.1.call-start = ((), (), s32[]{:S(2)}) async-start(), calls=%async_computation.4 | async-start | bytes 12582912 | tf_op jit(solution)/shard_map/reduce_scatter | solution.py:28
  82.6 2.6 %copy-start = (bf16[1024,512]{1,0:T(8,128)(2,1)S(1)}, bf16[1024,512]{1,0:T(8,128)(2,1)}, u32[]{:S(2)}) copy-start(bf16[1024,512]{1,0:T(8,128)(2,1)} %get-tuple-element.8) | copy-start | bytes 3145732
Sparse Core Ops, SparseCore 0:
  20.1 39.2 all-gather.1
  102.6 112.6 reduce-scatter.1
